TPU v7x, 32 devices: a whole 2x2x4 slice. The times are simulated.
32 devices in a mesh: wide: 8 (over z, x), narrow: 4 (over y, core).
Axes of the slice: x: 2, y: 2, z: 4, core: 2. Of those that a mesh axis runs over, the one named last changes fastest.
Arguments:
- tokens: bfloat16 [24, 512, 768], P('wide', 'narrow'), may hold values from -6 to 6
- lengths: int32 [24], P('wide'), may hold values from 1 to 512, as said below
- qkv_weight: bfloat16 [768, 2304], replicated, may hold values from -0.21875 to 0.21875
- qv_bias: float32 [2, 768], replicated, may hold values from -3 to 3
- out_weight: bfloat16 [768, 768], replicated, may hold values from -0.875 to 0.875
- out_bias: float32 [768], replicated, may hold values from -2 to 2
- norm1_gain: float32 [768], replicated, may hold values from 0.25 to 1.75
- norm1_shift: float32 [768], replicated, may hold values from -2 to 2
- up_weight: bfloat16 [768, 3072], replicated, may hold values from -0.21875 to 0.21875
- up_bias: float32 [3072], replicated, may hold values from -3 to 3
- down_weight: bfloat16 [3072, 768], replicated, may hold values from -0.109375 to 0.109375
- down_bias: float32 [768], replicated, may hold values from -2 to 2
- norm2_gain: float32 [768], replicated, may hold values from 0.25 to 1.75
- norm2_shift: float32 [768], replicated, may hold values from -2 to 2
- cotangent: bfloat16 [24, 512, 768], P('wide', 'narrow'), may hold values from -6 to 6
Outputs:
- output: bfloat16 [24, 512, 768], P('wide', 'narrow')
- input_grad: bfloat16 [24, 512, 768], P('wide', 'narrow')
- qkv_weight_grad: float32 [768, 2304], P('narrow')
- qv_bias_grad: float32 [2, 768], P(None, 'narrow')
- out_weight_grad: float32 [768, 768], P('narrow')
- out_bias_grad: float32 [768], P('narrow')
- norm1_gain_grad: float32 [768], P('narrow')
- norm1_shift_grad: float32 [768], P('narrow')
- up_weight_grad: float32 [768, 3072], P('narrow')
- up_bias_grad: float32 [3072], P('narrow')
- down_weight_grad: float32 [3072, 768], P('narrow')
- down_bias_grad: float32 [768], P('narrow')
- norm2_gain_grad: float32 [768], P('narrow')
- norm2_shift_grad: float32 [768], P('narrow')
Inputs may be any that keep to these rules, and one draw needn't show every extreme that they name: The slots of one group of 3 (aligned blocks) share a bucket b from 1 to 4, with lengths from (b - 1) * 128 + 1 to b * 128; slot 0 has length 512.
All inputs are finite; a program needn't handle non-finite values.
Results may differ from a plain program's by a relative error of at most 0.014.
Values may be sent and summed in bfloat16 or wider, within the bound.
A program may use at most 192 MiB of HBM per device.

v0:
```python
import jax
import jax.numpy as jnp
from jax import lax
from jax.sharding import PartitionSpec as P

H = 12
HD = 64
epsilon = 1e-12
root_half = 0.7071067811865476
inv_root_two_pi = 0.3989422804014327


def norm_forward(values, norm_gain, norm_shift):
    center = values - jnp.mean(values, axis=-1, keepdims=True)
    row_scale = lax.rsqrt(jnp.mean(center * center, axis=-1, keepdims=True) + epsilon)
    normed = center * row_scale
    return (normed * norm_gain + norm_shift, normed, row_scale)


def norm_backward(upstream, normed, row_scale, norm_gain):
    gain_grad = jnp.sum(upstream * normed, axis=0)
    shift_grad = jnp.sum(upstream, axis=0)
    scaled = upstream * norm_gain
    inner = scaled - jnp.mean(scaled, axis=-1, keepdims=True)
    inner = inner - normed * jnp.mean(scaled * normed, axis=-1, keepdims=True)
    return (row_scale * inner, gain_grad, shift_grad)


def split_packed(packed_seq):
    head_size = packed_seq.shape[2] // 3
    return (
        packed_seq[:, :, :head_size],
        packed_seq[:, :, head_size : 2 * head_size],
        packed_seq[:, :, 2 * head_size :],
    )


def masked_scores(query_part, key_part, length):
    raw_scores = jnp.einsum(
        "qhe,khe->hqk", query_part, key_part, preferred_element_type=jnp.float32
    )
    live_keys = lax.iota(jnp.int32, key_part.shape[0]) < length
    return jnp.where(live_keys[None, None, :], raw_scores * 0.125, -1000000000.0)


def attend(packed_seq, length):
    query_part, key_part, value_part = split_packed(packed_seq)
    scores = masked_scores(query_part, key_part, length)
    row_max = jnp.max(scores, axis=-1, keepdims=True)
    exponent = jnp.exp(scores - row_max)
    row_total = jnp.sum(exponent, axis=-1, keepdims=True)
    low_probs = (exponent / row_total).astype(jnp.bfloat16)
    context = jnp.einsum("hqk,khe->qhe", low_probs, value_part, preferred_element_type=jnp.float32)
    logsum = row_max + jnp.log(row_total)
    return (context.astype(jnp.bfloat16), logsum[:, :, 0])


def attend_backward(packed_seq, length, logsum, d_context):
    query_part, key_part, value_part = split_packed(packed_seq)
    scores = masked_scores(query_part, key_part, length)
    attn_probs = jnp.exp(scores - logsum[:, :, None])
    low_probs = attn_probs.astype(jnp.bfloat16)
    d_values = jnp.einsum("hqk,qhe->khe", low_probs, d_context, preferred_element_type=jnp.float32)
    d_probs = jnp.einsum("qhe,khe->hqk", d_context, value_part, preferred_element_type=jnp.float32)
    row_dot = jnp.sum(attn_probs * d_probs, axis=-1, keepdims=True)
    d_raw = (attn_probs * (d_probs - row_dot) * 0.125).astype(jnp.bfloat16)
    d_query = jnp.einsum("hqk,khe->qhe", d_raw, key_part, preferred_element_type=jnp.float32)
    d_keys = jnp.einsum("hqk,qhe->khe", d_raw, query_part, preferred_element_type=jnp.float32)
    return jnp.concatenate([d_query, d_keys, d_values], axis=-1).astype(jnp.bfloat16)


def local(
    tokens,
    lengths,
    qkv_weight,
    qv_bias,
    out_weight,
    out_bias,
    norm1_gain,
    norm1_shift,
    up_weight,
    up_bias,
    down_weight,
    down_bias,
    norm2_gain,
    norm2_shift,
    cotangent,
):
    groups, quarter, model_width = tokens.shape
    row_count = groups * quarter
    token_rows = tokens.reshape(row_count, model_width)
    zero_bias = jnp.zeros((H, HD), jnp.float32)
    bias_cols = jnp.stack([qv_bias[0].reshape(H, HD), zero_bias, qv_bias[1].reshape(H, HD)], axis=1)
    packed = jnp.dot(token_rows, qkv_weight, preferred_element_type=jnp.float32)
    packed = (packed + bias_cols.reshape(3 * model_width)).astype(jnp.bfloat16)
    packed = packed.reshape(groups, quarter, H, 3 * HD)
    head_parts = lax.all_to_all(packed, "narrow", split_axis=2, concat_axis=1, tiled=True)
    context, logsum = lax.map(lambda member: attend(member[0], member[1]), (head_parts, lengths))
    context_rows = lax.all_to_all(
        context, "narrow", split_axis=1, concat_axis=2, tiled=True
    ).reshape(row_count, model_width)
    attended = jnp.dot(context_rows, out_weight, preferred_element_type=jnp.float32) + out_bias
    first_norm, normed1, scale1 = norm_forward(
        token_rows.astype(jnp.float32) + attended, norm1_gain, norm1_shift
    )
    first_low = first_norm.astype(jnp.bfloat16)
    pre_act = jnp.dot(first_low, up_weight, preferred_element_type=jnp.float32) + up_bias
    erf_part = lax.erf(pre_act * root_half)
    activated = (0.5 * pre_act * (1.0 + erf_part)).astype(jnp.bfloat16)
    ffn_out = jnp.dot(activated, down_weight, preferred_element_type=jnp.float32) + down_bias
    result, normed2, scale2 = norm_forward(first_norm + ffn_out, norm2_gain, norm2_shift)
    output = result.astype(jnp.bfloat16).reshape(groups, quarter, model_width)
    positions = lax.axis_index("narrow") * quarter + lax.iota(jnp.int32, quarter)
    row_live = positions[None, :] < lengths[:, None]
    d_out = jnp.where(row_live[:, :, None], cotangent.astype(jnp.float32), 0.0).reshape(
        row_count, model_width
    )
    d_second, norm2_gain_grad, norm2_shift_grad = norm_backward(d_out, normed2, scale2, norm2_gain)
    d_ffn = d_second.astype(jnp.bfloat16)
    down_weight_grad = jnp.einsum("rf,rd->fd", activated, d_ffn, preferred_element_type=jnp.float32)
    down_bias_grad = jnp.sum(d_ffn.astype(jnp.float32), axis=0)
    d_activated = jnp.einsum("rd,fd->rf", d_ffn, down_weight, preferred_element_type=jnp.float32)
    slope = 0.5 * (1.0 + erf_part) + pre_act * jnp.exp(-0.5 * pre_act * pre_act) * inv_root_two_pi
    d_pre = (d_activated * slope).astype(jnp.bfloat16)
    up_weight_grad = jnp.einsum("rd,rf->df", first_low, d_pre, preferred_element_type=jnp.float32)
    up_bias_grad = jnp.sum(d_pre.astype(jnp.float32), axis=0)
    d_first = d_second + jnp.einsum(
        "rf,df->rd", d_pre, up_weight, preferred_element_type=jnp.float32
    )
    d_sum1, norm1_gain_grad, norm1_shift_grad = norm_backward(d_first, normed1, scale1, norm1_gain)
    d_att = d_sum1.astype(jnp.bfloat16)
    out_weight_grad = jnp.einsum(
        "rd,re->de", context_rows, d_att, preferred_element_type=jnp.float32
    )
    out_bias_grad = jnp.sum(d_att.astype(jnp.float32), axis=0)
    d_context = jnp.einsum("re,de->rd", d_att, out_weight, preferred_element_type=jnp.float32)
    d_context = d_context.astype(jnp.bfloat16).reshape(groups, quarter, H, HD)
    d_heads = lax.all_to_all(d_context, "narrow", split_axis=2, concat_axis=1, tiled=True)
    d_packed = lax.map(
        lambda member: attend_backward(member[0], member[1], member[2], member[3]),
        (head_parts, lengths, logsum, d_heads),
    )
    d_packed = lax.all_to_all(d_packed, "narrow", split_axis=1, concat_axis=2, tiled=True).reshape(
        row_count, 3 * model_width
    )
    qkv_weight_grad = jnp.einsum(
        "rd,rc->dc", token_rows, d_packed, preferred_element_type=jnp.float32
    )
    column_sums = jnp.sum(d_packed.astype(jnp.float32), axis=0).reshape(H, 3, HD)
    qv_bias_grad = jnp.stack(
        [column_sums[:, 0].reshape(model_width), column_sums[:, 2].reshape(model_width)]
    )
    d_input = d_sum1 + jnp.einsum(
        "rc,dc->rd", d_packed, qkv_weight, preferred_element_type=jnp.float32
    )
    input_grad = d_input.astype(jnp.bfloat16).reshape(groups, quarter, model_width)
    every_share = (
        lax.psum_scatter(qkv_weight_grad, "narrow", scatter_dimension=0, tiled=True),
        lax.psum_scatter(qv_bias_grad, "narrow", scatter_dimension=1, tiled=True),
        lax.psum_scatter(out_weight_grad, "narrow", scatter_dimension=0, tiled=True),
        lax.psum_scatter(out_bias_grad, "narrow", scatter_dimension=0, tiled=True),
        lax.psum_scatter(norm1_gain_grad, "narrow", scatter_dimension=0, tiled=True),
        lax.psum_scatter(norm1_shift_grad, "narrow", scatter_dimension=0, tiled=True),
        lax.psum_scatter(up_weight_grad, "narrow", scatter_dimension=0, tiled=True),
        lax.psum_scatter(up_bias_grad, "narrow", scatter_dimension=0, tiled=True),
        lax.psum_scatter(down_weight_grad, "narrow", scatter_dimension=0, tiled=True),
        lax.psum_scatter(down_bias_grad, "narrow", scatter_dimension=0, tiled=True),
        lax.psum_scatter(norm2_gain_grad, "narrow", scatter_dimension=0, tiled=True),
        lax.psum_scatter(norm2_shift_grad, "narrow", scatter_dimension=0, tiled=True),
    )
    every_total = lax.psum(
        (
            every_share[0],
            every_share[1],
            every_share[2],
            every_share[3],
            every_share[4],
            every_share[5],
            every_share[6],
            every_share[7],
            every_share[8],
            every_share[9],
            every_share[10],
            every_share[11],
        ),
        "wide",
    )
    return (
        output,
        input_grad,
        every_total[0],
        every_total[1],
        every_total[2],
        every_total[3],
        every_total[4],
        every_total[5],
        every_total[6],
        every_total[7],
        every_total[8],
        every_total[9],
        every_total[10],
        every_total[11],
    )


def solution(mesh):
    return jax.shard_map(
        local,
        mesh=mesh,
        in_specs=(
            P("wide", "narrow", None),
            P("wide"),
            P(),
            P(),
            P(),
            P(),
            P(),
            P(),
            P(),
            P(),
            P(),
            P(),
            P(),
            P(),
            P("wide", "narrow", None),
        ),
        out_specs=(
            P("wide", "narrow", None),
            P("wide", "narrow", None),
            P("narrow", None),
            P(None, "narrow"),
            P("narrow", None),
            P("narrow"),
            P("narrow"),
            P("narrow"),
            P("narrow", None),
            P("narrow"),
            P("narrow", None),
            P("narrow"),
            P("narrow"),
            P("narrow"),
        ),
        check_vma=False,
    )
```

profile of v0, /device:TPU:0, one launch (start us, length us, event | category | flops | bytes accessed | tf_op | source)
XLA Modules:
  0.0 858.6 jit_solution(15880051272732677894)
XLA Ops:
  11.1 3.8 fusion.66
  14.9 5.8 reshape.237
  20.7 4.7 copy.68
  25.4 4.5 all-to-all-start
  30.0 22.8 %all-to-all-done = bf16[3,128,12,192]{1,3,0,2:T(8,128)(2,1)} async-done(((bf16[3,128,12,192]{1,3,0,2:T(8,128)(2,1)}), bf16[3,128,12,192]{1,3,0,2:T(8,128)(2,1)}, u32[]{:S(2)}, u32[]{:S(2)}) %all-to-all-start) | async-done | bytes 1769504 | tf_op jit(solution)/shard_map/all_to_all | solution.py:97
  52.8 4.1 copy.70
  56.9 4.0 all_to_all.51
  60.9 18.2 %while.22 = (s32[]{:T(128)}, bf16[3,512,3,64]{1,3,2,0:T(8,128)(2,1)}, f32[3,3,512]{2,1,0:T(4,128)}, bf16[3,512,3,192]{1,3,2,0:T(8,128)(2,1)}, s32[3]{0:T(128)S(1)}, /*index=5*/s32[]{:T(128)}) while((s32[]{:T(128)}, bf16[3,512,3,64]{1,3,2,0:T(8,128)(2,1)}, f32[3,3,512]{2,1,0:T(4,128)}, bf16[3,512,3,192]{1,3,2,0:T(8,128)(2,1)}, s32[3]{0:T(128)S(1)}, ...), condition=%wide.region_3.4_spmd, body=%wide.region_0.3_spmd.sunk | while | flops 210861056 | bytes 11460713 | solution.py:98
  79.1 3.4 copy.71
  82.5 3.9 reshape.255
  86.4 4.6 all-to-all-start.1
  91.0 2.9 fusion.85
  94.6 6.1 all-to-all-done.1
  100.6 3.9 reshape.256
  104.5 4.0 copy.72
  111.5 4.4 multiply_convert_fusion.1
  122.4 4.1 convert_reduce_fusion
  126.4 2.9 multiply_reduce_fusion.1
  132.9 2.8 reshape.238
  138.3 4.2 all-to-all-start.2
  142.7 9.4 %all-to-all-done.2 = bf16[3,128,12,64]{1,3,0,2:T(8,128)(2,1)} async-done(((bf16[3,128,12,64]{1,3,0,2:T(8,128)(2,1)}), bf16[3,128,12,64]{1,3,0,2:T(8,128)(2,1)}, u32[]{:S(2)}, u32[]{:S(2)}) %all-to-all-start.2) | async-done | bytes 589856 | tf_op jit(solution)/shard_map/all_to_all | solution.py:138
  156.7 71.6 %while.23 = (s32[]{:T(128)}, bf16[3,512,3,192]{1,3,2,0:T(8,128)(2,1)}, bf16[3,512,3,192]{1,3,2,0:T(8,128)(2,1)}, s32[3]{0:T(128)}, f32[3,3,512]{2,1,0:T(4,128)}, /*index=5*/bf16[3,512,3,64]{1,3,2,0:T(8,128)(2,1)}, s32[]{:T(128)}) while((s32[]{:T(128)}, bf16[3,512,3,192]{1,3,2,0:T(8,128)(2,1)}, bf16[3,512,3,192]{1,3,2,0:T(8,128)(2,1)}, ...), condition=%wide.region_14.15_spmd, body=%wide.region_12.14_spmd.sunk | while | flops 516395520 | bytes 56251596 | solution.py:139
  165.7 6.4 fusion.147
  172.2 6.4 fusion.146
  189.6 6.4 fusion.147
  196.0 6.4 fusion.146
  213.4 6.4 fusion.147
  219.9 6.4 fusion.146
  228.2 5.6 copy.77
  233.8 42.2 %all_to_all.66 = bf16[3,512,3,192]{3,2,0,1:T(4,128)(2,1)} all-to-all(bf16[3,512,3,192]{3,2,0,1:T(4,128)(2,1)} %copy.77), channel_id=1, replica_groups=mesh['wide'=8,'narrow'=4] {'narrow'}, dimensions={1} | all-to-all | bytes 3538944 | tf_op jit(solution)/shard_map/all_to_all | solution.py:143
  276.0 7.2 copy.78
  283.2 6.7 convolution_bitcast_fusion
  289.9 8.0 copy.90
  298.0 3.7 fusion.82
  301.8 9.9 %fusion.93 = f32[768,3072]{1,0:T(8,128)} fusion(bf16[384,3072]{1,0:T(8,128)(2,1)} %copy-done.10, f32[384,768]{1,0:T(8,128)} %copy-done.5, f32[768]{0:T(1024)S(1)} %copy-done.13, f32[768]{0:T(1024)S(1)} %copy-done.12, f32[384]{0:T(512)S(1)} %add_rsqrt_fusion.1, f32[384]{0:T(512)S(1)} %broadcast_multiply_fusion.4), kind=kOutput, calls=%fused_computation.130 | convolution fusion | flops 1813413888 | bytes 12985344 | tf_op jit(solution)/shard_map/rd,rf->df/dot_general | solution.py:125
  312.0 8.5 fusion.90
  320.6 7.5 convert_reduce_fusion.1
  332.1 30.8 %reduce-scatter.16.cloned.1.call-done = f32[192,2304]{1,0:T(8,128)} async-done(((f32[768,2304]{1,0:T(8,128)}), f32[192,2304]{1,0:T(8,128)}) %reduce-scatter.16.cloned.1.call-update) | async-done | bytes 1769488
  362.9 2.9 copy.91
  365.9 32.9 %reduce-scatter.10.cloned.1.call-done = f32[192,768]{1,0:T(8,128)} async-done(((f32[768,768]{1,0:T(8,128)}), f32[192,768]{1,0:T(8,128)}) %reduce-scatter.10.cloned.1.call-update) | async-done | bytes 589840 | tf_op jit(solution)/shard_map/reduce_scatter | solution.py:160
  398.7 81.1 %reduce-scatter.12.cloned.1.call-done = f32[192,3072]{1,0:T(8,128)} async-done(((f32[768,3072]{1,0:T(8,128)}), f32[192,3072]{1,0:T(8,128)}) %reduce-scatter.12.cloned.1.call-update) | async-done | bytes 2359312 | tf_op jit(solution)/shard_map/reduce_scatter | solution.py:164
  479.8 80.9 %reduce-scatter.14.cloned.1.call-done = f32[768,768]{1,0:T(8,128)} async-done(((f32[3072,768]{1,0:T(8,128)}), f32[768,768]{1,0:T(8,128)}) %reduce-scatter.14.cloned.1.call-update) | async-done | bytes 2359312 | tf_op jit(solution)/shard_map/reduce_scatter | solution.py:166
  563.3 11.1 %all-reduce.9 = (f32[768]{0:T(1024)}, f32[768]{0:T(1024)}, f32[768]{0:T(1024)}, f32[3072]{0:T(1024)}, f32[768]{0:T(1024)}, /*index=5*/f32[768]{0:T(1024)}, f32[768]{0:T(1024)}) all-reduce(f32[768]{0:T(1024)S(1)} %copy-done.19, f32[768]{0:T(1024)} %get-tuple-element.135, ...), channel_id=5, replica_groups=mesh['wide'=8,'narrow'=4] {'narrow'}, use_global_device_ids=true, to_apply=%region_23.24.clone | all-reduce | flops 7680 | bytes 61440
  581.9 4.4 fusion.75
  587.3 38.8 %all-reduce.7 = (f32[2,192]{1,0:T(2,128)}, f32[192]{0:T(256)}, f32[192]{0:T(256)}, f32[192]{0:T(256)}, f32[768]{0:T(1024)}, /*index=5*/f32[192]{0:T(256)}, f32[192]{0:T(256)}, f32[192]{0:T(256)}) all-reduce(f32[2,192]{1,0:T(2,128)S(1)} %copy.93, f32[192]{0:T(256)S(1)} %dynamic-slice.1, ...), channel_id=1, replica_groups=mesh['wide'=8,'narrow'=4] {'wide'}, use_global_device_ids=true, to_apply=%region_19.20 | all-reduce | flops 2304 | bytes 18432 | tf_op jit(solution)/shard_map/psum | solution.py:171
  626.1 215.7 %all-reduce.12.cloned.1.call-done = (f32[192,2304]{0,1:T(8,128)}, f32[192,768]{1,0:T(8,128)}, f32[192,3072]{1,0:T(8,128)}, f32[768,768]{1,0:T(8,128)}) async-done(((f32[192,2304]{0,1:T(8,128)}, f32[192,768]{1,0:T(8,128)}, f32[192,3072]{1,0:T(8,128)}, f32[768,768]{1,0:T(8,128)}), (f32[192,2304]{0,1:T(8,128)}, f32[192,768]{1,0:T(8,128)}, f32[192,3072]{1,0:T(8,128)}, ...) | async-done | bytes 7077904 | tf_op jit(solution)/shard_map/psum | solution.py:171
  841.8 2.9 copy.79
  846.6 3.4 copy.139
  (179 shorter events, 93.4 us)
Async XLA Ops:
  7.2 3.9 copy-start
  25.4 4.6 copy-start.25
  25.4 27.4 %all-to-all-start = ((bf16[3,128,12,192]{1,3,0,2:T(8,128)(2,1)}), bf16[3,128,12,192]{1,3,0,2:T(8,128)(2,1)}, u32[]{:S(2)}, u32[]{:S(2)}) async-start(bf16[3,128,12,192]{1,3,0,2:T(8,128)(2,1)} %copy.68), calls=%async_computation | async-start | bytes 3538944 | tf_op jit(solution)/shard_map/all_to_all | solution.py:97
  82.5 8.5 copy-start.14
  86.4 14.2 %all-to-all-start.1 = ((bf16[4,2,36864]{2,1,0:T(2,128)(2,1)}), bf16[4,2,36864]{2,1,0:T(2,128)(2,1)}, u32[]{:S(2)}, u32[]{:S(2)}) async-start(bf16[4,2,36864]{2,1,0:T(2,128)(2,1)} %reshape.255), calls=%async_computation.1 | async-start | bytes 1179648 | tf_op jit(solution)/shard_map/all_to_all | solution.py:99
  94.6 14.0 %copy-start.23 = (f32[768]{0:T(1024)S(1)}, f32[768]{0:T(1024)}, u32[]{:S(2)}) copy-start(f32[768]{0:T(1024)} %param.24) | copy-start | bytes 9220
  108.5 2.9 copy-start.12
  108.5 2.9 copy-start.13
  108.5 2.9 copy-start.22
  108.5 7.3 slice-start
  111.1 18.2 %copy-start.5 = (f32[384,768]{1,0:T(8,128)}, f32[384,768]{1,0:T(8,128)S(1)}, u32[]{:S(2)}) copy-start(f32[384,768]{1,0:T(8,128)S(1)} %get-tuple-element.195) | copy-start | bytes 3538948
  111.5 4.5 slice-start.1
  111.5 4.4 copy-start.24
  115.9 2.2 copy-start.8
  115.9 2.5 copy-start.15
  118.1 1.3 copy-start.4
  118.1 2.3 copy-start.20
  118.2 2.3 copy-start.21
  120.4 6.0 slice-start.2
  122.4 4.1 copy-start.7
  122.4 4.1 slice-start.3
  126.4 2.9 copy-start.10
  129.4 2.0 copy-start.11
  130.4 1.0 copy-start.6
  138.3 13.8 %all-to-all-start.2 = ((bf16[3,128,12,64]{1,3,0,2:T(8,128)(2,1)}), bf16[3,128,12,64]{1,3,0,2:T(8,128)(2,1)}, u32[]{:S(2)}, u32[]{:S(2)}) async-start(bf16[3,128,12,64]{1,3,0,2:T(8,128)(2,1)} %copy.74), calls=%async_computation.2 | async-start | bytes 1179648 | tf_op jit(solution)/shard_map/all_to_all | solution.py:138
  142.5 220.4 %reduce-scatter.16.cloned.1.call-start = ((), (), s32[]{:S(2)}) async-start(), calls=%async_computation.12 | async-start | bytes 8847360
  160.4 3.0 copy-start.2
  160.4 1.3 copy-start.3
  161.7 1.7 copy-start.1
  184.2 3.0 copy-start.2
  184.2 1.3 copy-start.3
  185.5 1.7 copy-start.1
  208.1 3.0 copy-start.2
  208.1 1.3 copy-start.3
  209.4 1.7 copy-start.1
  298.0 100.8 %reduce-scatter.10.cloned.1.call-start = ((), (), s32[]{:S(2)}) async-start(), calls=%async_computation.9 | async-start | bytes 2949120 | tf_op jit(solution)/shard_map/reduce_scatter | solution.py:160
  301.7 178.1 %reduce-scatter.12.cloned.1.call-start = ((), (), s32[]{:S(2)}) async-start(), calls=%async_computation.10 | async-start | bytes 11796480 | tf_op jit(solution)/shard_map/reduce_scatter | solution.py:164
  311.7 249.0 %reduce-scatter.14.cloned.1.call-start = ((), (), s32[]{:S(2)}) async-start(), calls=%async_computation.11 | async-start | bytes 11796480 | tf_op jit(solution)/shard_map/reduce_scatter | solution.py:166
  320.6 265.8 %reduce-scatter.18.cloned.1.call-start = ((), (), s32[]{:S(2)}) async-start(), calls=%async_computation.13 | async-start | bytes 491520
  332.1 509.8 %all-reduce.12.cloned.1.call-start = ((), (), s32[]{:S(2)}) async-start(), calls=%async_computation.14 | async-start | bytes 15335424 | tf_op jit(solution)/shard_map/psum | solution.py:171
  560.7 2.6 copy-start.16
  560.7 2.6 copy-start.17
  560.7 2.6 copy-start.18
  560.7 2.6 copy-start.19
  846.6 3.5 copy-start.9
Sparse Core Ops, SparseCore 0:
  298.1 64.7 reduce-scatter.15
  365.6 33.0 reduce-scatter.9
  401.3 78.4 reduce-scatter.11
  482.3 78.3 reduce-scatter.13
  563.6 20.7 reduce-scatter.17
  589.4 252.3 all-reduce.11
where the time goes:
time: 867 us; the launch traced here: 859 us
  waiting for transfers between devices  480 us (55%)
  matrix products  115 us (13%)
  local copies, waits for them, and re-layouts  111 us (13%)
  blocking collectives  92.1 us (11%)
  other arithmetic  30 us (3%)
  between operations  16 us (2%)
  starting transfers between devices  13.9 us (2%)
    psum x1, waiting for transfers between devices, local(): lax.psum((every_share[0], every_share[1], every_share[2], every_share[3],...  216 us
    reduce_scatter x1, waiting for transfers between devices, local(): lax.psum_scatter(up_weight_grad, 'narrow', scatter_dimension=0, tiled=True)  81.1 us
    reduce_scatter x1, waiting for transfers between devices, local(): lax.psum_scatter(down_weight_grad, 'narrow', scatter_dimension=0, tiled=T...  80.9 us
    all_to_all x1, blocking collectives, local(): lax.all_to_all(d_packed, 'narrow', split_axis=1, concat_axis=2, tiled=True)  42.2 us
    unnamed x72, local copies, waits for them, and re-layouts  41.2 us
    psum x1, blocking collectives, local(): lax.psum((every_share[0], every_share[1], every_share[2], every_share[3],...  38.8 us
    reduce_scatter x1, waiting for transfers between devices, local(): lax.psum_scatter(out_weight_grad, 'narrow', scatter_dimension=0, tiled=True)  32.9 us
    unnamed x8, waiting for transfers between devices  30.9 us
  transfers between devices with their start and end apart: 9, of which 8 were waited for; matrix products, arithmetic and copies ran while one was open for 6% of the time, Pallas kernels for 0%

commit v1 on v0

--- a/solution.py
+++ b/solution.py
@@ -8,6 +8,29 @@
 epsilon = 1e-12
 root_half = 0.7071067811865476
 inv_root_two_pi = 0.3989422804014327
+
+
+def split_up(array, dim, length):
+    shape = array.shape
+    blocks = array.reshape(*shape[:dim], length, shape[dim] // length, *shape[dim + 1 :])
+    return jnp.moveaxis(blocks, dim, 0)
+
+
+def in_order(tiles, dim):
+    shape = list(tiles.shape[1:])
+    shape[dim] *= tiles.shape[0]
+    return jnp.moveaxis(tiles, 0, dim).reshape(shape)
+
+
+def swapped_with_each(shard, axis, split_dim, concat_dim):
+    count, here = (lax.axis_size(axis), lax.axis_index(axis))
+    blocks = split_up(shard, split_dim, count)
+    done = [blocks[here]]
+    for turn in range(1, count):
+        sent = blocks[here ^ turn]
+        done.append(lax.ppermute(sent, axis, [(i, i ^ turn) for i in range(count)]))
+    blocks = jnp.stack(done)[here ^ jnp.arange(count)]
+    return in_order(blocks, concat_dim)
 
 
 def norm_forward(values, norm_gain, norm_shift):
@@ -135,7 +158,7 @@
     out_bias_grad = jnp.sum(d_att.astype(jnp.float32), axis=0)
     d_context = jnp.einsum("re,de->rd", d_att, out_weight, preferred_element_type=jnp.float32)
     d_context = d_context.astype(jnp.bfloat16).reshape(groups, quarter, H, HD)
-    d_heads = lax.all_to_all(d_context, "narrow", split_axis=2, concat_axis=1, tiled=True)
+    d_heads = swapped_with_each(d_context, "narrow", 2, 1)
     d_packed = lax.map(
         lambda member: attend_backward(member[0], member[1], member[2], member[3]),
         (head_parts, lengths, logsum, d_heads),

time: 867 us -> 868 us (level)
    all_to_all x1 -> x0, waiting for transfers between devices: 9.38 us -> none  [local(): lax.all_to_all(d_context, 'narrow', split_axis=2, concat_axis=1, tiled=True)]
  transfers between devices with their start and end apart: 9 -> 11, of which waited for: 8 -> 9; matrix products, arithmetic and copies ran while one was open for 6% -> 7% of each run, Pallas kernels for 0% -> 0%
where the time goes in v1:
time: 868 us; the launch traced here: 859 us
  waiting for transfers between devices  475 us (55%)
  local copies, waits for them, and re-layouts  116 us (13%)
  matrix products  115 us (13%)
  blocking collectives  92.1 us (11%)
  other arithmetic  33.7 us (4%)
  between operations  16.1 us (2%)
  starting transfers between devices  11.5 us (1%)
    psum x1, waiting for transfers between devices, local(): lax.psum((every_share[0], every_share[1], every_share[2], every_share[3],...  216 us
    reduce_scatter x1, waiting for transfers between devices, local(): lax.psum_scatter(up_weight_grad, 'narrow', scatter_dimension=0, tiled=True)  81.1 us
    reduce_scatter x1, waiting for transfers between devices, local(): lax.psum_scatter(down_weight_grad, 'narrow', scatter_dimension=0, tiled=T...  80.9 us
    all_to_all x1, blocking collectives, local(): lax.all_to_all(d_packed, 'narrow', split_axis=1, concat_axis=2, tiled=True)  42.2 us
    unnamed x72, local copies, waits for them, and re-layouts  41.2 us
    psum x1, blocking collectives, local(): lax.psum((every_share[0], every_share[1], every_share[2], every_share[3],...  38.8 us
    reduce_scatter x1, waiting for transfers between devices, local(): lax.psum_scatter(out_weight_grad, 'narrow', scatter_dimension=0, tiled=True)  32.9 us
    unnamed x8, waiting for transfers between devices  30.9 us
  transfers between devices with their start and end apart: 11, of which 9 were waited for; matrix products, arithmetic and copies ran while one was open for 7% of the time, Pallas kernels for 0%

profile of v1, /device:TPU:0, one launch (start us, length us, event | category | flops | bytes accessed | tf_op | source)
XLA Modules:
  0.0 859.4 jit_solution(7734831447610549822)
XLA Ops:
  11.1 3.8 fusion.66
  14.9 5.8 reshape.268
  20.7 4.7 copy.73
  25.4 4.5 all-to-all-start
  30.1 22.8 %all-to-all-done = bf16[3,128,12,192]{1,3,0,2:T(8,128)(2,1)} async-done(((bf16[3,128,12,192]{1,3,0,2:T(8,128)(2,1)}), bf16[3,128,12,192]{1,3,0,2:T(8,128)(2,1)}, u32[]{:S(2)}, u32[]{:S(2)}) %all-to-all-start) | async-done | bytes 1769504 | tf_op jit(solution)/shard_map/all_to_all | solution.py:120
  52.8 4.1 copy.75
  56.9 4.0 all_to_all.38
  60.9 18.2 %while.22 = (s32[]{:T(128)}, bf16[3,512,3,64]{1,3,2,0:T(8,128)(2,1)}, f32[3,3,512]{2,1,0:T(4,128)}, bf16[3,512,3,192]{1,3,2,0:T(8,128)(2,1)}, s32[3]{0:T(128)S(1)}, /*index=5*/s32[]{:T(128)}) while((s32[]{:T(128)}, bf16[3,512,3,64]{1,3,2,0:T(8,128)(2,1)}, f32[3,3,512]{2,1,0:T(4,128)}, bf16[3,512,3,192]{1,3,2,0:T(8,128)(2,1)}, s32[3]{0:T(128)S(1)}, ...), condition=%wide.region_3.4_spmd, body=%wide.region_0.3_spmd.sunk | while | flops 210861056 | bytes 11460713 | solution.py:121
  79.1 3.4 copy.76
  82.5 3.9 reshape.285
  86.4 4.1 all-to-all-start.1
  91.1 2.9 fusion.85
  94.6 5.6 all-to-all-done.1
  100.2 3.9 reshape.286
  104.0 4.0 copy.77
  108.1 2.6 fusion.97
  111.0 4.4 multiply_convert_fusion.1
  121.9 4.1 convert_reduce_fusion
  126.0 2.9 multiply_reduce_fusion.1
  134.5 2.6 reshape_reshape.3
  152.7 2.6 gather_fusion
  157.3 71.7 %while.23 = (s32[]{:T(128)}, bf16[3,512,3,192]{1,3,2,0:T(8,128)(2,1)}, bf16[3,512,3,192]{1,3,2,0:T(8,128)(2,1)}, s32[3]{0:T(128)}, f32[3,3,512]{2,1,0:T(4,128)}, /*index=5*/bf16[3,512,3,64]{1,3,2,0:T(8,128)(2,1)}, s32[]{:T(128)}) while((s32[]{:T(128)}, bf16[3,512,3,192]{1,3,2,0:T(8,128)(2,1)}, bf16[3,512,3,192]{1,3,2,0:T(8,128)(2,1)}, ...), condition=%wide.region_14.15_spmd, body=%wide.region_12.14_spmd.sunk | while | flops 516395520 | bytes 56251596 | solution.py:162
  166.5 6.4 fusion.149
  173.0 6.4 fusion.148
  190.4 6.4 fusion.149
  196.8 6.4 fusion.148
  214.2 6.4 fusion.149
  220.7 6.4 fusion.148
  229.0 5.6 copy.84
  234.6 42.2 %all_to_all.48 = bf16[3,512,3,192]{3,2,0,1:T(4,128)(2,1)} all-to-all(bf16[3,512,3,192]{3,2,0,1:T(4,128)(2,1)} %copy.84), channel_id=1, replica_groups=mesh['wide'=8,'narrow'=4] {'narrow'}, dimensions={1} | all-to-all | bytes 3538944 | tf_op jit(solution)/shard_map/all_to_all | solution.py:166
  276.8 7.2 copy.85
  284.0 6.7 convolution_bitcast_fusion
  290.7 8.0 copy.94
  298.8 3.7 fusion.82
  302.6 9.9 %fusion.94 = f32[768,3072]{1,0:T(8,128)} fusion(bf16[384,3072]{1,0:T(8,128)(2,1)} %copy-done.10, f32[384,768]{1,0:T(8,128)} %copy-done.5, f32[768]{0:T(1024)S(1)} %copy-done.13, f32[768]{0:T(1024)S(1)} %copy-done.12, f32[384]{0:T(512)S(1)} %add_rsqrt_fusion.1, f32[384]{0:T(512)S(1)} %broadcast_multiply_fusion.4), kind=kOutput, calls=%fused_computation.144 | convolution fusion | flops 1813413888 | bytes 12985344 | tf_op jit(solution)/shard_map/rd,rf->df/dot_general | solution.py:148
  312.8 8.5 fusion.91
  321.4 7.5 convert_reduce_fusion.1
  332.9 30.8 %reduce-scatter.16.cloned.1.call-done = f32[192,2304]{1,0:T(8,128)} async-done(((f32[768,2304]{1,0:T(8,128)}), f32[192,2304]{1,0:T(8,128)}) %reduce-scatter.16.cloned.1.call-update) | async-done | bytes 1769488
  363.7 2.9 copy.95
  366.7 32.9 %reduce-scatter.10.cloned.1.call-done = f32[192,768]{1,0:T(8,128)} async-done(((f32[768,768]{1,0:T(8,128)}), f32[192,768]{1,0:T(8,128)}) %reduce-scatter.10.cloned.1.call-update) | async-done | bytes 589840 | tf_op jit(solution)/shard_map/reduce_scatter | solution.py:183
  399.5 81.1 %reduce-scatter.12.cloned.1.call-done = f32[192,3072]{1,0:T(8,128)} async-done(((f32[768,3072]{1,0:T(8,128)}), f32[192,3072]{1,0:T(8,128)}) %reduce-scatter.12.cloned.1.call-update) | async-done | bytes 2359312 | tf_op jit(solution)/shard_map/reduce_scatter | solution.py:187
  480.6 80.9 %reduce-scatter.14.cloned.1.call-done = f32[768,768]{1,0:T(8,128)} async-done(((f32[3072,768]{1,0:T(8,128)}), f32[768,768]{1,0:T(8,128)}) %reduce-scatter.14.cloned.1.call-update) | async-done | bytes 2359312 | tf_op jit(solution)/shard_map/reduce_scatter | solution.py:189
  564.1 11.1 %all-reduce.9 = (f32[768]{0:T(1024)}, f32[768]{0:T(1024)}, f32[768]{0:T(1024)}, f32[3072]{0:T(1024)}, f32[768]{0:T(1024)}, /*index=5*/f32[768]{0:T(1024)}, f32[768]{0:T(1024)}) all-reduce(f32[768]{0:T(1024)S(1)} %copy-done.19, f32[768]{0:T(1024)} %get-tuple-element.135, ...), channel_id=5, replica_groups=mesh['wide'=8,'narrow'=4] {'narrow'}, use_global_device_ids=true, to_apply=%region_23.24.clone | all-reduce | flops 7680 | bytes 61440
  582.7 4.4 fusion.75
  588.1 38.8 %all-reduce.7 = (f32[2,192]{1,0:T(2,128)}, f32[192]{0:T(256)}, f32[192]{0:T(256)}, f32[192]{0:T(256)}, f32[768]{0:T(1024)}, /*index=5*/f32[192]{0:T(256)}, f32[192]{0:T(256)}, f32[192]{0:T(256)}) all-reduce(f32[2,192]{1,0:T(2,128)S(1)} %copy.97, f32[192]{0:T(256)S(1)} %dynamic-slice.17, ...), channel_id=1, replica_groups=mesh['wide'=8,'narrow'=4] {'wide'}, use_global_device_ids=true, to_apply=%region_19.20 | all-reduce | flops 2304 | bytes 18432 | tf_op jit(solution)/shard_map/psum | solution.py:194
  626.9 215.7 %all-reduce.12.cloned.1.call-done = (f32[192,2304]{0,1:T(8,128)}, f32[192,768]{1,0:T(8,128)}, f32[192,3072]{1,0:T(8,128)}, f32[768,768]{1,0:T(8,128)}) async-done(((f32[192,2304]{0,1:T(8,128)}, f32[192,768]{1,0:T(8,128)}, f32[192,3072]{1,0:T(8,128)}, f32[768,768]{1,0:T(8,128)}), (f32[192,2304]{0,1:T(8,128)}, f32[192,768]{1,0:T(8,128)}, f32[192,3072]{1,0:T(8,128)}, ...) | async-done | bytes 7077904 | tf_op jit(solution)/shard_map/psum | solution.py:194
  842.6 2.9 copy.86
  847.4 3.4 copy.153
  (191 shorter events, 103.5 us)
Async XLA Ops:
  7.2 3.9 copy-start
  25.4 4.6 copy-start.25
  25.4 27.4 %all-to-all-start = ((bf16[3,128,12,192]{1,3,0,2:T(8,128)(2,1)}), bf16[3,128,12,192]{1,3,0,2:T(8,128)(2,1)}, u32[]{:S(2)}, u32[]{:S(2)}) async-start(bf16[3,128,12,192]{1,3,0,2:T(8,128)(2,1)} %copy.73), calls=%async_computation | async-start | bytes 3538944 | tf_op jit(solution)/shard_map/all_to_all | solution.py:120
  82.5 8.6 copy-start.14
  86.4 13.8 %all-to-all-start.1 = ((bf16[4,2,36864]{2,1,0:T(2,128)(2,1)}), bf16[4,2,36864]{2,1,0:T(2,128)(2,1)}, u32[]{:S(2)}, u32[]{:S(2)}) async-start(bf16[4,2,36864]{2,1,0:T(2,128)(2,1)} %reshape.285), calls=%async_computation.1 | async-start | bytes 1179648 | tf_op jit(solution)/shard_map/all_to_all | solution.py:122
  90.6 273.2 %reduce-scatter.16.cloned.1.call-start = ((), (), s32[]{:S(2)}) async-start(), calls=%async_computation.11 | async-start | bytes 8847360
  94.6 13.5 %copy-start.23 = (f32[768]{0:T(1024)S(1)}, f32[768]{0:T(1024)}, u32[]{:S(2)}) copy-start(f32[768]{0:T(1024)} %param.24) | copy-start | bytes 9220
  108.1 2.9 copy-start.12
  108.1 2.9 copy-start.13
  108.1 2.9 copy-start.22
  108.1 7.3 slice-start
  110.7 18.2 %copy-start.5 = (f32[384,768]{1,0:T(8,128)}, f32[384,768]{1,0:T(8,128)S(1)}, u32[]{:S(2)}) copy-start(f32[384,768]{1,0:T(8,128)S(1)} %get-tuple-element.199) | copy-start | bytes 3538948
  111.0 4.5 slice-start.1
  111.0 4.4 copy-start.24
  115.4 2.2 copy-start.8
  115.5 2.5 copy-start.15
  117.7 1.3 copy-start.4
  117.7 2.3 copy-start.20
  117.7 2.3 copy-start.21
  120.0 6.0 slice-start.2
  121.9 4.1 copy-start.7
  121.9 4.1 slice-start.3
  126.0 2.9 copy-start.10
  128.9 2.0 copy-start.11
  129.9 1.0 copy-start.6
  141.4 4.6 collective-permute-start
  141.4 7.0 collective-permute-start.1
  141.8 9.0 %collective-permute-start.2 = (bf16[3,128,3,64]{1,3,2,0:T(8,128)(2,1)}, bf16[3,128,3,64]{1,3,2,0:T(8,128)(2,1)}, u32[]{:S(2)}, u32[]{:S(2)}) collective-permute-start(bf16[3,128,3,64]{1,3,2,0:T(8,128)(2,1)} %bitcast.126), channel_id=1, source_target_pairs={{0,3},{1,2},{2,1},{3,0},{4,7},{5,6},{6,5},{7,4},{8,11},{9,10},{10,... | collective-permute-start | bytes 442376 | tf_op jit(solution)/shard_map/ppermute | solution.py:31
  161.2 3.0 copy-start.2
  161.2 1.3 copy-start.3
  162.5 1.7 copy-start.1
  185.0 3.0 copy-start.2
  185.0 1.3 copy-start.3
  186.3 1.7 copy-start.1
  208.9 3.0 copy-start.2
  208.9 1.3 copy-start.3
  210.2 1.7 copy-start.1
  298.8 100.8 %reduce-scatter.10.cloned.1.call-start = ((), (), s32[]{:S(2)}) async-start(), calls=%async_computation.8 | async-start | bytes 2949120 | tf_op jit(solution)/shard_map/reduce_scatter | solution.py:183
  302.5 178.1 %reduce-scatter.12.cloned.1.call-start = ((), (), s32[]{:S(2)}) async-start(), calls=%async_computation.9 | async-start | bytes 11796480 | tf_op jit(solution)/shard_map/reduce_scatter | solution.py:187
  312.5 249.0 %reduce-scatter.14.cloned.1.call-start = ((), (), s32[]{:S(2)}) async-start(), calls=%async_computation.10 | async-start | bytes 11796480 | tf_op jit(solution)/shard_map/reduce_scatter | solution.py:189
  321.4 265.8 %reduce-scatter.18.cloned.1.call-start = ((), (), s32[]{:S(2)}) async-start(), calls=%async_computation.12 | async-start | bytes 491520
  332.9 509.8 %all-reduce.12.cloned.1.call-start = ((), (), s32[]{:S(2)}) async-start(), calls=%async_computation.13 | async-start | bytes 15335424 | tf_op jit(solution)/shard_map/psum | solution.py:194
  561.5 2.6 copy-start.16
  561.5 2.6 copy-start.17
  561.5 2.6 copy-start.18
  561.5 2.6 copy-start.19
  847.4 3.5 copy-start.9
Sparse Core Ops, SparseCore 0:
  298.9 64.7 reduce-scatter.15
  366.4 33.0 reduce-scatter.9
  402.1 78.4 reduce-scatter.11
  483.1 78.3 reduce-scatter.13
  564.4 20.7 reduce-scatter.17
  590.2 252.3 all-reduce.11
